TPU v7x, 32 devices: a whole 2x2x4 slice. The times are simulated.
32 devices in a mesh: group: 2 (over y), dev: 8 (over z, x), tp: 2 (over core).
Axes of the slice: x: 2, y: 2, z: 4, core: 2. Of those that a mesh axis runs over, the one named last changes fastest.
Arguments:
- prompt_activations: bfloat16 [4096, 8192], P(('group', 'dev')), parts along dimension 0, may hold values from -6 to 6
- key_matrix: bfloat16 [8192, 512], P('dev', 'tp'), may hold values from -0.0625 to 0.0625
- value_matrix: bfloat16 [8192, 512], P('dev', 'tp'), may hold values from -0.0625 to 0.0625
- adapter_down_keyvalue: bfloat16 [8192, 128], P('dev'), may hold values from -0.0625 to 0.0625
- adapter_up_key: bfloat16 [64, 512], P(None, 'tp'), may hold values from -1.5 to 1.5
- adapter_up_value: bfloat16 [64, 512], P(None, 'tp'), may hold values from -1.5 to 1.5
- request_adapter: int32 [16], P('group'), parts along dimension 0, may hold values from 0 to 3
- page_request: int32 [1024, 1], P('group'), parts along dimension 0, may hold values from 0 to 7; in each aligned block of 64 rows (0 to 63, 64 to 127, ...) at most 8 rows name the same one
- context_tokens: int32 [16], P('group'), parts along dimension 0, may hold values from 64 to 256
- step_query: bfloat16 [16, 4096], P(('group', 'dev'), 'tp'), parts along dimension 0, may hold values from -256 to 256
- step_key: bfloat16 [16, 512], P(('group', 'dev'), 'tp'), parts along dimension 0, may hold values from -6 to 6
- step_value: bfloat16 [16, 512], P(('group', 'dev'), 'tp'), parts along dimension 0, may hold values from -6 to 6
- stored_keys: bfloat16 [16, 256, 512], P(('group', 'dev'), None, 'tp'), parts along dimension 0, may hold values from -6 to 6
- stored_values: bfloat16 [16, 256, 512], P(('group', 'dev'), None, 'tp'), parts along dimension 0, may hold values from -6 to 6
- output_matrix: bfloat16 [4096, 8192], P('tp', 'dev'), may hold values from -0.09375 to 0.09375
- adapter_down_output: bfloat16 [4096, 64], P('tp'), may hold values from -0.09375 to 0.09375
- adapter_up_output: bfloat16 [64, 8192], P(None, 'dev'), may hold values from -1.5 to 1.5
Outputs:
- attended: bfloat16 [16, 8192], P('group', 'dev'), parts along dimension 0
There are 2 independent parts, one for each index of `group`. A program takes and returns all parts, laid end to end along the dimension named above; an argument that names none is the same for every part. Nothing has to cross between parts.
Inputs may be any that keep to these rules, and one draw needn't show every extreme that they name: `page_request`: among the pages of one device's prompt block (aligned blocks of 64 pages), no request owns more than 8; every request owns at least one page.
All inputs are finite; a program needn't handle non-finite values.
Results may differ from a plain program's by a relative error of at most 0.0086.
Values may be sent and summed in bfloat16 or wider, within the bound.
A program may use at most 64 MiB of HBM per device.

v0:
```python
import jax
import jax.numpy as jnp
from jax import lax
from jax.sharding import PartitionSpec as P

HEADS = 32
KV_HEADS = 4
HEAD = 128
LOW_RANK = 16
ADAPTER_COUNT = 4
PAGE = 4
adapter_scale = 1.0
rope_base = 500000.0


def rotate(key_rows, positions):
    row_count = key_rows.shape[0]
    blocks = key_rows.reshape(row_count, -1, HEAD)
    half_size = HEAD // 2
    exponent = jnp.arange(half_size, dtype=jnp.float32) * (2.0 / HEAD)
    frequency = jnp.exp(-jnp.log(jnp.float32(rope_base)) * exponent)
    angles = positions.astype(jnp.float32)[:, None] * frequency[None, :]
    cosine = jnp.cos(angles)[:, None, :]
    sine_part = jnp.sin(angles)[:, None, :]
    first_half = blocks[..., :half_size]
    second_half = blocks[..., half_size:]
    turned = jnp.concatenate(
        [
            first_half * cosine - second_half * sine_part,
            second_half * cosine + first_half * sine_part,
        ],
        axis=-1,
    )
    return turned.reshape(row_count, -1)


def owner_ranks(owners, row_total):
    onehot = (owners[:, None] == jnp.arange(row_total, dtype=jnp.int32)[None, :]).astype(jnp.int32)
    before = jnp.cumsum(onehot, axis=0) - onehot
    rank = jnp.sum(before * onehot, axis=1)
    return (onehot, rank)


def mask_columns(narrowed, adapter_list):
    column = jnp.arange(narrowed.shape[1], dtype=jnp.int32)
    owner = column % (ADAPTER_COUNT * LOW_RANK) // LOW_RANK
    return jnp.where(owner[None, :] == adapter_list[:, None], narrowed, jnp.zeros_like(narrowed))


def selected_narrow(activation_rows, adapter_down, adapter_list):
    narrowed = jnp.dot(activation_rows, adapter_down, preferred_element_type=jnp.float32)
    return mask_columns(narrowed, adapter_list)


def widened(selected_rows, up_key, up_value):
    split_at = ADAPTER_COUNT * LOW_RANK
    highest = lax.Precision.HIGHEST
    key_portion = jnp.dot(
        selected_rows[:, :split_at], up_key.astype(jnp.float32), precision=highest
    )
    value_portion = jnp.dot(
        selected_rows[:, split_at:], up_value.astype(jnp.float32), precision=highest
    )
    return (adapter_scale * key_portion, adapter_scale * value_portion)


def attend_local(
    query,
    old_keys,
    old_values,
    old_length,
    fresh_keys,
    fresh_values,
    fresh_valid,
    last_key,
    last_value,
):
    group_size = HEADS // KV_HEADS
    query_heads = query.reshape(-1, group_size, HEAD)
    kv_local = query_heads.shape[0]
    scale_factor = HEAD ** (-0.5)

    def score_of(key_rows):
        shaped = key_rows.reshape(key_rows.shape[0], kv_local, HEAD)
        return (
            jnp.einsum("kgd,lkd->kgl", query_heads, shaped, preferred_element_type=jnp.float32)
            * scale_factor
        )

    def mix_with(probs, value_rows):
        shaped = value_rows.reshape(value_rows.shape[0], kv_local, HEAD)
        return jnp.einsum("kgl,lkd->kgd", probs, shaped, preferred_element_type=jnp.float32)

    old_valid = jnp.arange(old_keys.shape[0], dtype=jnp.int32) < old_length
    old_scores = jnp.where(old_valid[None, None, :], score_of(old_keys), -1e30)
    fresh_scores = jnp.where(fresh_valid[None, None, :], score_of(fresh_keys), -1e30)
    last_score = score_of(last_key[None, :])
    top = jnp.maximum(
        jnp.maximum(
            jnp.max(old_scores, axis=-1, keepdims=True),
            jnp.max(fresh_scores, axis=-1, keepdims=True),
        ),
        last_score,
    )
    old_weights = jnp.exp(old_scores - top)
    fresh_weights = jnp.exp(fresh_scores - top)
    last_weight = jnp.exp(last_score - top)
    total = (
        jnp.sum(old_weights, axis=-1, keepdims=True)
        + jnp.sum(fresh_weights, axis=-1, keepdims=True)
        + last_weight
    )
    output = mix_with((old_weights / total).astype(jnp.bfloat16), old_values)
    output = output + mix_with((fresh_weights / total).astype(jnp.bfloat16), fresh_values)
    output = output + mix_with((last_weight / total).astype(jnp.bfloat16), last_value[None, :])
    return output.reshape(-1).astype(jnp.bfloat16)


def per_device(
    prompt_activations,
    key_matrix,
    value_matrix,
    adapter_down_keyvalue,
    adapter_up_key,
    adapter_up_value,
    request_adapter,
    page_request,
    context_tokens,
    step_query,
    step_key,
    step_value,
    stored_keys,
    stored_values,
    output_matrix,
    adapter_down_output,
    adapter_up_output,
):
    devices = lax.axis_size("dev")
    device = lax.axis_index("dev")
    tok_count = prompt_activations.shape[0]
    pages_here = tok_count // PAGE
    capacity = max(2, (pages_here + devices - 1) // devices)
    row_total = request_adapter.shape[0]
    owners = page_request[:, 0]
    onehot, rank = owner_ranks(owners, row_total)
    first_page = device * pages_here
    my_owners = lax.dynamic_slice_in_dim(owners, first_page, pages_here, 0)
    my_rank = lax.dynamic_slice_in_dim(rank, first_page, pages_here, 0)
    tokens = jnp.arange(tok_count, dtype=jnp.int32)
    token_page = tokens // PAGE
    token_owner = jnp.take(my_owners, token_page)
    position = (
        jnp.take(context_tokens, token_owner) + jnp.take(my_rank, token_page) * PAGE + tokens % PAGE
    )
    adapter_list = jnp.take(request_adapter, token_owner)
    key_width = key_matrix.shape[1]

    def add_rows(portion):
        return jnp.dot(prompt_activations, portion, preferred_element_type=jnp.float32)

    key_raw = add_rows(lax.all_gather(key_matrix, "dev", axis=0, tiled=True))
    value_raw = add_rows(lax.all_gather(value_matrix, "dev", axis=0, tiled=True))
    down_complete = lax.all_gather(adapter_down_keyvalue, "dev", axis=0, tiled=True)
    narrowed = jnp.dot(prompt_activations, down_complete, preferred_element_type=jnp.float32)
    selected_rows = mask_columns(narrowed, adapter_list)
    key_delta, value_delta = widened(selected_rows, adapter_up_key, adapter_up_value)
    key_rows = rotate(key_raw + key_delta, position).astype(jnp.bfloat16)
    value_rows = (value_raw + value_delta).astype(jnp.bfloat16)
    joined_rows = jnp.concatenate([key_rows, value_rows], axis=1)
    local_hot = (my_owners[:, None] == jnp.arange(row_total, dtype=jnp.int32)[None, :]).astype(
        jnp.int32
    )
    local_before = jnp.cumsum(local_hot, axis=0) - local_hot
    local_slot = jnp.sum(local_before * local_hot, axis=1)
    peer_slots = capacity * PAGE
    target = token_owner * peer_slots + jnp.take(local_slot, token_page) * PAGE + tokens % PAGE
    outgoing = (
        jnp.zeros((devices * peer_slots, 2 * key_width), jnp.bfloat16).at[target].set(joined_rows)
    )
    outgoing = outgoing.reshape(devices, peer_slots, 2 * key_width)
    incoming = lax.all_to_all(outgoing, "dev", split_axis=0, concat_axis=0, tiled=True)
    fresh_keys = incoming[:, :, :key_width].reshape(-1, key_width)
    fresh_values = incoming[:, :, key_width:].reshape(-1, key_width)
    my_column = jnp.take(onehot, device, axis=1)
    count_from = jnp.sum(my_column.reshape(devices, pages_here), axis=1)
    slot_page = jnp.arange(peer_slots, dtype=jnp.int32) // PAGE
    fresh_valid = (slot_page[None, :] < count_from[:, None]).reshape(-1)
    mixed_local = attend_local(
        step_query[0],
        stored_keys[0],
        stored_values[0],
        jnp.take(context_tokens, device),
        fresh_keys,
        fresh_values,
        fresh_valid,
        step_key[0],
        step_value[0],
    ).reshape(1, -1)
    portion = lax.all_gather(mixed_local, "dev", axis=0, tiled=True)
    plain_result = jnp.dot(portion, output_matrix, preferred_element_type=jnp.float32)
    selected_output = selected_narrow(portion, adapter_down_output, request_adapter)
    partial_output = plain_result + adapter_scale * jnp.dot(
        selected_output, adapter_up_output.astype(jnp.float32), precision=lax.Precision.HIGHEST
    )
    return lax.psum(partial_output, "tp").astype(jnp.bfloat16)


def solution(mesh):
    return jax.shard_map(
        per_device,
        mesh=mesh,
        in_specs=(
            P(("group", "dev"), None),
            P("dev", "tp"),
            P("dev", "tp"),
            P("dev", None),
            P(None, "tp"),
            P(None, "tp"),
            P("group"),
            P("group", None),
            P("group"),
            P(("group", "dev"), "tp"),
            P(("group", "dev"), "tp"),
            P(("group", "dev"), "tp"),
            P(("group", "dev"), None, "tp"),
            P(("group", "dev"), None, "tp"),
            P("tp", "dev"),
            P("tp", None),
            P(None, "dev"),
        ),
        out_specs=P("group", "dev"),
        check_vma=False,
    )
```

profile of v0, /device:TPU:0, one launch (start us, length us, event | category | flops | bytes accessed | tf_op | source)
XLA Modules:
  0.0 273.4 jit_solution(10275499087581960177)
XLA Ops:
  6.5 0.7 all-gather.7.cloned.1.call-update
  7.3 0.7 all-gather.9.cloned.1.call-update
  8.1 0.7 all-gather.5.cloned.1.call-update
  8.8 0.7 fusion.22
  9.4 1.1 reduce-window.6
  10.8 0.8 fusion.20
  11.7 0.7 dynamic-slice_bitcast_fusion
  12.4 1.9 gather_fusion
  14.3 1.9 gather_fusion.2
  16.2 0.7 fusion.21
  17.4 1.9 gather_fusion.1
  21.4 9.7 %fusion.41 = (f32[256]{0:T(256)S(1)}, s32[256]{0:T(256)S(1)}, s32[256]{0:T(256)S(1)}) fusion(s32[256]{0:T(256)S(1)} %gather_fusion.2, s32[]{:T(128)} %bitcast.19, s32[]{:T(128)} %bitcast.18, s32[]{:T(128)} %bitcast.17, s32[]{:T(128)} %bitcast.16, s32[]{:T(128)} %bitcast.15, s32[]{:T(128)} %bitcast.14, s32[]{:T(128)} %bitcast.13, s32[]{:T(128)} %bitcast.12, ...), kind=kLoop, calls=%fused_computation.94 | loop fusion | flops 15616 | bytes 6208 | tf_op jit(solution)/shard_map/convert_element_type | solution.py:22
  31.4 29.8 %all-gather.7.cloned.1.call-done = bf16[8192,128]{1,0:T(8,128)(2,1)} async-done(((bf16[1024,128]{1,0:T(8,128)(2,1)}), bf16[8192,128]{1,0:T(8,128)(2,1)}) %all-gather.7.cloned.1.call-update) | async-done | bytes 2097168 | tf_op jit(solution)/shard_map/all_gather | solution.py:163
  61.3 4.4 %convolution_select_fusion = f32[256,128]{0,1:T(8,128)S(1)} fusion(bf16[256,8192]{1,0:T(8,128)(2,1)} %param.21, bf16[8192,128]{1,0:T(8,128)(2,1)} %all-gather.7.cloned.1.call-done, s32[256]{0:T(256)S(1)} %get-tuple-element.40, s32[128]{0:T(128)S(1)} %and_select_fusion.2), kind=kOutput, calls=%fused_computation.7 | convolution fusion | flops 536936448 | bytes 6424064 | tf_op jit(solution)/shard_map/dot_general | solution.py:164
  65.6 69.1 %all-gather.9.cloned.1.call-done = bf16[8192,256]{1,0:T(8,128)(2,1)} async-done(((bf16[1024,256]{1,0:T(8,128)(2,1)}), bf16[8192,256]{1,0:T(8,128)(2,1)}) %all-gather.9.cloned.1.call-update) | async-done | bytes 4194320 | tf_op jit(solution)/shard_map/all_gather | solution.py:162
  134.7 5.2 %fusion.51 = f32[256,256]{0,1:T(8,128)S(1)} fusion(bf16[256,8192]{1,0:T(8,128)(2,1)} %param.21, bf16[8192,256]{1,0:T(8,128)(2,1)} %all-gather.9.cloned.1.call-done), kind=kOutput, calls=%fused_computation.123 | convolution fusion | flops 1073741824 | bytes 8650752 | tf_op jit(solution)/shard_map/dot_general | solution.py:159
  140.3 67.9 %all-gather.5.cloned.1.call-done = bf16[8192,256]{1,0:T(8,128)(2,1)} async-done(((bf16[1024,256]{1,0:T(8,128)(2,1)}), bf16[8192,256]{1,0:T(8,128)(2,1)}) %all-gather.5.cloned.1.call-update) | async-done | bytes 4194320 | tf_op jit(solution)/shard_map/all_gather | solution.py:161
  208.2 5.2 %fusion.50 = f32[256,256]{0,1:T(8,128)S(1)} fusion(bf16[256,8192]{1,0:T(8,128)(2,1)} %param.21, bf16[8192,256]{1,0:T(8,128)(2,1)} %all-gather.5.cloned.1.call-done), kind=kOutput, calls=%fused_computation.122 | convolution fusion | flops 1073741824 | bytes 8650752 | tf_op jit(solution)/shard_map/dot_general | solution.py:159
  214.0 2.2 scatter_custom_fusion
  216.2 3.4 %all-to-all-start = ((bf16[8,32,512]{2,1,0:T(8,128)(2,1)}), bf16[8,32,512]{2,1,0:T(8,128)(2,1)S(1)}, u32[]{:S(2)}, u32[]{:S(2)}) async-start(bf16[8,32,512]{2,1,0:T(8,128)(2,1)} %bitcast.24), calls=%async_computation | async-start | bytes 524288 | tf_op jit(solution)/shard_map/all_to_all | solution.py:181
  220.2 8.0 %all-to-all-done = bf16[8,32,512]{2,1,0:T(8,128)(2,1)S(1)} async-done(((bf16[8,32,512]{2,1,0:T(8,128)(2,1)}), bf16[8,32,512]{2,1,0:T(8,128)(2,1)S(1)}, u32[]{:S(2)}, u32[]{:S(2)}) %all-to-all-start) | async-done | bytes 262176 | tf_op jit(solution)/shard_map/all_to_all | solution.py:181
  229.2 30.5 %all-gather = bf16[8,1,2048]{2,1,0:T(2,128)(2,1)S(1)} all-gather(bf16[1,1,2048]{2,1,0:T(2,128)(2,1)S(1)} %reshape.342), channel_id=1, replica_groups=mesh['group'=2,'dev'=8,'tp'=2] {'dev'}, dimensions={0}, use_global_device_ids=true | all-gather | bytes 36864 | tf_op jit(solution)/shard_map/all_gather | solution.py:199
  259.7 2.8 %fusion.16 = f32[8,1024]{1,0:T(8,128)S(1)} fusion(bf16[2048,1024]{1,0:T(8,128)(2,1)} %param.35, bf16[8,1,2048]{2,1,0:T(2,128)(2,1)S(1)} %all-gather), kind=kOutput, calls=%fused_computation.34 | convolution fusion | flops 33554432 | bytes 4259840 | tf_op jit(solution)/shard_map/dot_general | solution.py:200
  262.9 4.0 %psum.7 = bf16[8,1024]{1,0:T(8,128)(2,1)} all-reduce(f32[8,1024]{1,0:T(8,128)S(1)} %convolution_add_fusion.2), channel_id=1, replica_groups=mesh['group'=2,'dev'=8,'tp'=2] {'tp'}, use_global_device_ids=true, to_apply=%region_11.14 | all-reduce | flops 8192 | bytes 49152 | tf_op jit(solution)/shard_map/psum | solution.py:205
  (71 shorter events, 5.5 us)
Async XLA Ops:
  6.5 256.0 %copy-start = (bf16[2048,64]{0,1:T(8,128)(2,1)S(1)}, bf16[2048,64]{0,1:T(8,128)(2,1)}, u32[]{:S(2)}) copy-start(bf16[2048,64]{0,1:T(8,128)(2,1)} %param.36) | copy-start | bytes 786436
  6.5 12.8 %copy-start.4 = (s32[8]{0:T(128)S(1)}, s32[8]{0:T(128)}, u32[]{:S(2)}) copy-start(s32[8]{0:T(128)} %param.29) | copy-start | bytes 100
  6.5 14.1 %copy-start.6 = (s32[8]{0:T(128)S(1)}, s32[8]{0:T(128)}, u32[]{:S(2)}) copy-start(s32[8]{0:T(128)} %param.27) | copy-start | bytes 100
  6.5 54.7 %all-gather.7.cloned.1.call-start = ((), (), s32[]{:S(2)}) async-start(), calls=%async_computation.2 | async-start | bytes 2359296 | tf_op jit(solution)/shard_map/all_gather | solution.py:163
  7.3 127.5 %all-gather.9.cloned.1.call-start = ((), (), s32[]{:S(2)}) async-start(), calls=%async_computation.3 | async-start | bytes 4718592 | tf_op jit(solution)/shard_map/all_gather | solution.py:162
  8.0 200.2 %all-gather.5.cloned.1.call-start = ((), (), s32[]{:S(2)}) async-start(), calls=%async_computation.1 | async-start | bytes 4718592 | tf_op jit(solution)/shard_map/all_gather | solution.py:161
  65.6 74.3 %copy-start.7 = (bf16[64,256]{1,0:T(8,128)(2,1)S(1)}, bf16[64,256]{1,0:T(8,128)(2,1)}, u32[]{:S(2)}) copy-start(bf16[64,256]{1,0:T(8,128)(2,1)} %param.26) | copy-start | bytes 98308
  140.3 73.2 %copy-start.5 = (bf16[64,256]{1,0:T(8,128)(2,1)S(1)}, bf16[64,256]{1,0:T(8,128)(2,1)}, u32[]{:S(2)}) copy-start(bf16[64,256]{1,0:T(8,128)(2,1)} %param.25) | copy-start | bytes 98308
  140.3 79.3 %copy-start.9 = (bf16[1,256]{1,0:T(2,128)(2,1)S(1)}, bf16[1,256]{1,0:T(2,128)(2,1)}, u32[]{:S(2)}) copy-start(bf16[1,256]{1,0:T(2,128)(2,1)} %param.32) | copy-start | bytes 1540
  140.3 79.4 %copy-start.1 = (bf16[1,256,256]{2,1,0:T(8,128)(2,1)S(1)}, bf16[1,256,256]{2,1,0:T(8,128)(2,1)}, u32[]{:S(2)}) copy-start(bf16[1,256,256]{2,1,0:T(8,128)(2,1)} %param.33) | copy-start | bytes 393220
  140.3 79.5 %copy-start.2 = (bf16[1,256,256]{2,1,0:T(8,128)(2,1)S(1)}, bf16[1,256,256]{2,1,0:T(8,128)(2,1)}, u32[]{:S(2)}) copy-start(bf16[1,256,256]{2,1,0:T(8,128)(2,1)} %param.34) | copy-start | bytes 393220
  140.3 79.5 %copy-start.8 = (bf16[1,2048]{1,0:T(2,128)(2,1)S(1)}, bf16[1,2048]{1,0:T(2,128)(2,1)}, u32[]{:S(2)}) copy-start(bf16[1,2048]{1,0:T(2,128)(2,1)} %param.30) | copy-start | bytes 12292
  140.3 79.5 %copy-start.10 = (bf16[1,256]{1,0:T(2,128)(2,1)S(1)}, bf16[1,256]{1,0:T(2,128)(2,1)}, u32[]{:S(2)}) copy-start(bf16[1,256]{1,0:T(2,128)(2,1)} %param.31) | copy-start | bytes 1540
  213.9 48.9 %copy-start.3 = (bf16[64,1024]{1,0:T(8,128)(2,1)S(1)}, bf16[64,1024]{1,0:T(8,128)(2,1)}, u32[]{:S(2)}) copy-start(bf16[64,1024]{1,0:T(8,128)(2,1)} %param.37) | copy-start | bytes 393220
  216.2 12.0 %all-to-all-start = ((bf16[8,32,512]{2,1,0:T(8,128)(2,1)}), bf16[8,32,512]{2,1,0:T(8,128)(2,1)S(1)}, u32[]{:S(2)}, u32[]{:S(2)}) async-start(bf16[8,32,512]{2,1,0:T(8,128)(2,1)} %bitcast.24), calls=%async_computation | async-start | bytes 524288 | tf_op jit(solution)/shard_map/all_to_all | solution.py:181
Sparse Core Ops, SparseCore 0:
  9.5 51.7 all-gather.6
  63.4 71.3 all-gather.8
  136.9 71.3 all-gather.4
where the time goes:
time: 274 us; the launch traced here: 273 us
  waiting for transfers between devices  177 us (65%)
  blocking collectives  34.5 us (13%)
  matrix products  19.5 us (7%)
  other arithmetic  14.3 us (5%)
  between operations  14 us (5%)
  local copies, waits for them, and re-layouts  10.7 us (4%)
  starting transfers between devices  3.49 us (1%)
    all_gather x1, waiting for transfers between devices, per_device(): lax.all_gather(value_matrix, 'dev', axis=0, tiled=True)  69.1 us
    all_gather x1, waiting for transfers between devices, per_device(): key_raw = add_rows(lax.all_gather(key_matrix, 'dev', axis=0, tiled=True))  67.9 us
    all_gather x1, blocking collectives, per_device(): portion = lax.all_gather(mixed_local, 'dev', axis=0, tiled=True)  30.5 us
    all_gather x1, waiting for transfers between devices, per_device(): lax.all_gather(adapter_down_keyvalue, 'dev', axis=0, tiled=True)  29.8 us
    dot_general x2, matrix products, add_rows(): jnp.dot(prompt_activations, portion, preferred_element_type=jnp.float32)  10.4 us
    convert_element_type x1, other arithmetic, rotate(): angles = positions.astype(jnp.float32)[:, None] * frequency[None, :]  9.74 us
    all_to_all x1, waiting for transfers between devices, per_device(): lax.all_to_all(outgoing, 'dev', split_axis=0, concat_axis=0, tiled=True)  8 us
  transfers between devices with their start and end apart: 4, of which 4 were waited for; matrix products, arithmetic and copies ran while one was open for 12% of the time, Pallas kernels for 0%

commit v1 on v0

--- a/solution.py
+++ b/solution.py
@@ -196,7 +196,12 @@
         step_key[0],
         step_value[0],
     ).reshape(1, -1)
-    portion = lax.all_gather(mixed_local, "dev", axis=0, tiled=True)
+    ring = [mixed_local]
+    for hop in range(7):
+        ring.append(lax.ppermute(ring[-1], "dev", [(dev, (dev + 1) % 8) for dev in range(8)]))
+    portion = jnp.roll(
+        jnp.concatenate(ring[::-1], axis=0), (lax.axis_index("dev") + 1) * ring[0].shape[0], axis=0
+    )
     plain_result = jnp.dot(portion, output_matrix, preferred_element_type=jnp.float32)
     selected_output = selected_narrow(portion, adapter_down_output, request_adapter)
     partial_output = plain_result + adapter_scale * jnp.dot(

time: 274 us -> 288 us (1.051)
  waiting for transfers between devices: 177 us -> 220 us
  blocking collectives: 34.5 us -> 3.98 us
    ppermute x0 -> x7, waiting for transfers between devices: none -> 43 us  [per_device(): lax.ppermute(ring[-1], 'dev', [(dev, (dev + 1) % 8) for dev in range(8)])]
    all_gather x1 -> x0, blocking collectives: 30.5 us -> none  [per_device(): portion = lax.all_gather(mixed_local, 'dev', axis=0, tiled=True)]
  transfers between devices with their start and end apart: 4 -> 11, of which waited for: 4 -> 11; matrix products, arithmetic and copies ran while one was open for 12% -> 11% of each run, Pallas kernels for 0% -> 0%
where the time goes in v1:
time: 288 us
  waiting for transfers between devices  220 us (76%)
  matrix products  19.5 us (7%)
  other arithmetic  14.3 us (5%)
  between operations  14 us (5%)
  local copies, waits for them, and re-layouts  10.9 us (4%)
  starting transfers between devices  4.97 us (2%)
  blocking collectives  3.98 us (1%)
    all_gather x1, waiting for transfers between devices, per_device(): lax.all_gather(value_matrix, 'dev', axis=0, tiled=True)  69.1 us
    all_gather x1, waiting for transfers between devices, per_device(): key_raw = add_rows(lax.all_gather(key_matrix, 'dev', axis=0, tiled=True))  67.9 us
    ppermute x7, waiting for transfers between devices, per_device(): lax.ppermute(ring[-1], 'dev', [(dev, (dev + 1) % 8) for dev in range(8)])  43 us
    all_gather x1, waiting for transfers between devices, per_device(): lax.all_gather(adapter_down_keyvalue, 'dev', axis=0, tiled=True)  29.8 us
    dot_general x2, matrix products, add_rows(): jnp.dot(prompt_activations, portion, preferred_element_type=jnp.float32)  10.4 us
    convert_element_type x1, other arithmetic, rotate(): angles = positions.astype(jnp.float32)[:, None] * frequency[None, :]  9.74 us
    all_to_all x1, waiting for transfers between devices, per_device(): lax.all_to_all(outgoing, 'dev', split_axis=0, concat_axis=0, tiled=True)  8 us
  transfers between devices with their start and end apart: 11, of which 11 were waited for; matrix products, arithmetic and copies ran while one was open for 11% of the time, Pallas kernels for 0%

profile of v1, /device:TPU:0, one launch (start us, length us, event | category | flops | bytes accessed | tf_op | source)
XLA Modules:
  0.0 287.6 jit_solution(12283344256710790057)
XLA Ops:
  9.4 1.1 reduce-window.6
  12.4 1.9 gather_fusion
  14.3 1.9 gather_fusion.2
  17.4 1.9 gather_fusion.1
  21.4 9.7 %fusion.38 = (f32[256]{0:T(256)S(1)}, s32[256]{0:T(256)S(1)}) fusion(s32[256]{0:T(256)S(1)} %gather_fusion.2, s32[]{:T(128)} %bitcast.19, s32[]{:T(128)} %bitcast.18, s32[]{:T(128)} %bitcast.17, s32[]{:T(128)} %bitcast.16, s32[]{:T(128)} %bitcast.15, s32[]{:T(128)} %bitcast.14, s32[]{:T(128)} %bitcast.13, s32[]{:T(128)} %bitcast.12, s32[256]{0:T(256)S(1)} %gather_fusion, ...), kind=kLoop, calls=%fused_computation.91 | loop fusion | flops 13568 | bytes 4160 | tf_op jit(solution)/shard_map/convert_element_type | solution.py:22
  31.4 29.8 %all-gather.6.cloned.1.call-done = bf16[8192,128]{1,0:T(8,128)(2,1)} async-done(((bf16[1024,128]{1,0:T(8,128)(2,1)}), bf16[8192,128]{1,0:T(8,128)(2,1)}) %all-gather.6.cloned.1.call-update) | async-done | bytes 2097168 | tf_op jit(solution)/shard_map/all_gather | solution.py:163
  61.3 4.4 %convolution_select_fusion = f32[256,128]{0,1:T(8,128)S(1)} fusion(bf16[256,8192]{1,0:T(8,128)(2,1)} %param.21, bf16[8192,128]{1,0:T(8,128)(2,1)} %all-gather.6.cloned.1.call-done, s32[256]{0:T(256)S(1)} %get-tuple-element.40, s32[128]{0:T(128)S(1)} %and_select_fusion.2), kind=kOutput, calls=%fused_computation.7 | convolution fusion | flops 536936448 | bytes 6424064 | tf_op jit(solution)/shard_map/dot_general | solution.py:164
  65.6 69.1 %all-gather.8.cloned.1.call-done = bf16[8192,256]{1,0:T(8,128)(2,1)} async-done(((bf16[1024,256]{1,0:T(8,128)(2,1)}), bf16[8192,256]{1,0:T(8,128)(2,1)}) %all-gather.8.cloned.1.call-update) | async-done | bytes 4194320 | tf_op jit(solution)/shard_map/all_gather | solution.py:162
  134.7 5.2 %fusion.51 = f32[256,256]{0,1:T(8,128)S(1)} fusion(bf16[256,8192]{1,0:T(8,128)(2,1)} %param.21, bf16[8192,256]{1,0:T(8,128)(2,1)} %all-gather.8.cloned.1.call-done), kind=kOutput, calls=%fused_computation.123 | convolution fusion | flops 1073741824 | bytes 8650752 | tf_op jit(solution)/shard_map/dot_general | solution.py:159
  140.3 67.9 %all-gather.4.cloned.1.call-done = bf16[8192,256]{1,0:T(8,128)(2,1)} async-done(((bf16[1024,256]{1,0:T(8,128)(2,1)}), bf16[8192,256]{1,0:T(8,128)(2,1)}) %all-gather.4.cloned.1.call-update) | async-done | bytes 4194320 | tf_op jit(solution)/shard_map/all_gather | solution.py:161
  208.2 5.2 %fusion.50 = f32[256,256]{0,1:T(8,128)S(1)} fusion(bf16[256,8192]{1,0:T(8,128)(2,1)} %param.21, bf16[8192,256]{1,0:T(8,128)(2,1)} %all-gather.4.cloned.1.call-done), kind=kOutput, calls=%fused_computation.122 | convolution fusion | flops 1073741824 | bytes 8650752 | tf_op jit(solution)/shard_map/dot_general | solution.py:159
  214.0 2.2 scatter_custom_fusion
  216.2 3.4 %all-to-all-start = ((bf16[8,32,512]{2,1,0:T(8,128)(2,1)}), bf16[8,32,512]{2,1,0:T(8,128)(2,1)S(1)}, u32[]{:S(2)}, u32[]{:S(2)}) async-start(bf16[8,32,512]{2,1,0:T(8,128)(2,1)} %bitcast.24), calls=%async_computation | async-start | bytes 524288 | tf_op jit(solution)/shard_map/all_to_all | solution.py:181
  220.2 8.0 %all-to-all-done = bf16[8,32,512]{2,1,0:T(8,128)(2,1)S(1)} async-done(((bf16[8,32,512]{2,1,0:T(8,128)(2,1)}), bf16[8,32,512]{2,1,0:T(8,128)(2,1)S(1)}, u32[]{:S(2)}, u32[]{:S(2)}) %all-to-all-start) | async-done | bytes 262176 | tf_op jit(solution)/shard_map/all_to_all | solution.py:181
  229.2 1.5 collective-permute-start
  230.6 4.9 %collective-permute-done = bf16[1,2048]{1,0:T(2,128)(2,1)S(1)} collective-permute-done((bf16[1,2048]{1,0:T(2,128)(2,1)S(1)}, bf16[1,2048]{1,0:T(2,128)(2,1)S(1)}, u32[]{:S(2)}, u32[]{:S(2)}) %collective-permute-start) | collective-permute-done | bytes 4128 | tf_op jit(solution)/shard_map/ppermute | solution.py:201
  235.6 6.3 %collective-permute-done.1 = bf16[1,2048]{1,0:T(2,128)(2,1)S(1)} collective-permute-done((bf16[1,2048]{1,0:T(2,128)(2,1)S(1)}, bf16[1,2048]{1,0:T(2,128)(2,1)S(1)}, u32[]{:S(2)}, u32[]{:S(2)}) %collective-permute-start.1) | collective-permute-done | bytes 4128 | tf_op jit(solution)/shard_map/ppermute | solution.py:201
  241.9 6.3 %collective-permute-done.2 = bf16[1,2048]{1,0:T(2,128)(2,1)S(1)} collective-permute-done((bf16[1,2048]{1,0:T(2,128)(2,1)S(1)}, bf16[1,2048]{1,0:T(2,128)(2,1)S(1)}, u32[]{:S(2)}, u32[]{:S(2)}) %collective-permute-start.2) | collective-permute-done | bytes 4128 | tf_op jit(solution)/shard_map/ppermute | solution.py:201
  248.3 6.3 %collective-permute-done.3 = bf16[1,2048]{1,0:T(2,128)(2,1)S(1)} collective-permute-done((bf16[1,2048]{1,0:T(2,128)(2,1)S(1)}, bf16[1,2048]{1,0:T(2,128)(2,1)S(1)}, u32[]{:S(2)}, u32[]{:S(2)}) %collective-permute-start.3) | collective-permute-done | bytes 4128 | tf_op jit(solution)/shard_map/ppermute | solution.py:201
  254.6 6.3 %collective-permute-done.4 = bf16[1,2048]{1,0:T(2,128)(2,1)S(1)} collective-permute-done((bf16[1,2048]{1,0:T(2,128)(2,1)S(1)}, bf16[1,2048]{1,0:T(2,128)(2,1)S(1)}, u32[]{:S(2)}, u32[]{:S(2)}) %collective-permute-start.4) | collective-permute-done | bytes 4128 | tf_op jit(solution)/shard_map/ppermute | solution.py:201
  261.0 6.3 %collective-permute-done.5 = bf16[1,2048]{1,0:T(2,128)(2,1)S(1)} collective-permute-done((bf16[1,2048]{1,0:T(2,128)(2,1)S(1)}, bf16[1,2048]{1,0:T(2,128)(2,1)S(1)}, u32[]{:S(2)}, u32[]{:S(2)}) %collective-permute-start.5) | collective-permute-done | bytes 4128 | tf_op jit(solution)/shard_map/ppermute | solution.py:201
  267.3 6.3 %collective-permute-done.6 = bf16[1,2048]{1,0:T(2,128)(2,1)S(1)} collective-permute-done((bf16[1,2048]{1,0:T(2,128)(2,1)S(1)}, bf16[1,2048]{1,0:T(2,128)(2,1)S(1)}, u32[]{:S(2)}, u32[]{:S(2)}) %collective-permute-start.6) | collective-permute-done | bytes 4128 | tf_op jit(solution)/shard_map/ppermute | solution.py:201
  274.2 2.9 convolution_add_fusion.2
  277.1 4.0 %psum.7 = bf16[8,1024]{1,0:T(8,128)(2,1)} all-reduce(f32[8,1024]{1,0:T(8,128)S(1)} %convolution_add_fusion.2), channel_id=1, replica_groups=mesh['group'=2,'dev'=8,'tp'=2] {'tp'}, use_global_device_ids=true, to_apply=%region_11.14 | all-reduce | flops 8192 | bytes 49152 | tf_op jit(solution)/shard_map/psum | solution.py:210
  (86 shorter events, 10.7 us)
Async XLA Ops:
  6.5 267.3 %copy-start = (bf16[2048,64]{0,1:T(8,128)(2,1)S(1)}, bf16[2048,64]{0,1:T(8,128)(2,1)}, u32[]{:S(2)}) copy-start(bf16[2048,64]{0,1:T(8,128)(2,1)} %param.36) | copy-start | bytes 786436
  6.5 12.8 %copy-start.5 = (s32[8]{0:T(128)S(1)}, s32[8]{0:T(128)}, u32[]{:S(2)}) copy-start(s32[8]{0:T(128)} %param.29) | copy-start | bytes 100
  6.5 14.1 %copy-start.4 = (s32[8]{0:T(128)S(1)}, s32[8]{0:T(128)}, u32[]{:S(2)}) copy-start(s32[8]{0:T(128)} %param.27) | copy-start | bytes 100
  6.5 54.7 %all-gather.6.cloned.1.call-start = ((), (), s32[]{:S(2)}) async-start(), calls=%async_computation.2 | async-start | bytes 2359296 | tf_op jit(solution)/shard_map/all_gather | solution.py:163
  7.3 127.5 %all-gather.8.cloned.1.call-start = ((), (), s32[]{:S(2)}) async-start(), calls=%async_computation.3 | async-start | bytes 4718592 | tf_op jit(solution)/shard_map/all_gather | solution.py:162
  8.0 200.2 %all-gather.4.cloned.1.call-start = ((), (), s32[]{:S(2)}) async-start(), calls=%async_computation.1 | async-start | bytes 4718592 | tf_op jit(solution)/shard_map/all_gather | solution.py:161
  65.6 74.3 %copy-start.7 = (bf16[64,256]{1,0:T(8,128)(2,1)S(1)}, bf16[64,256]{1,0:T(8,128)(2,1)}, u32[]{:S(2)}) copy-start(bf16[64,256]{1,0:T(8,128)(2,1)} %param.26) | copy-start | bytes 98308
  140.3 73.2 %copy-start.6 = (bf16[64,256]{1,0:T(8,128)(2,1)S(1)}, bf16[64,256]{1,0:T(8,128)(2,1)}, u32[]{:S(2)}) copy-start(bf16[64,256]{1,0:T(8,128)(2,1)} %param.25) | copy-start | bytes 98308
  140.3 79.3 %copy-start.9 = (bf16[1,256]{1,0:T(2,128)(2,1)S(1)}, bf16[1,256]{1,0:T(2,128)(2,1)}, u32[]{:S(2)}) copy-start(bf16[1,256]{1,0:T(2,128)(2,1)} %param.32) | copy-start | bytes 1540
  140.3 79.4 %copy-start.1 = (bf16[1,256,256]{2,1,0:T(8,128)(2,1)S(1)}, bf16[1,256,256]{2,1,0:T(8,128)(2,1)}, u32[]{:S(2)}) copy-start(bf16[1,256,256]{2,1,0:T(8,128)(2,1)} %param.33) | copy-start | bytes 393220
  140.3 79.5 %copy-start.2 = (bf16[1,256,256]{2,1,0:T(8,128)(2,1)S(1)}, bf16[1,256,256]{2,1,0:T(8,128)(2,1)}, u32[]{:S(2)}) copy-start(bf16[1,256,256]{2,1,0:T(8,128)(2,1)} %param.34) | copy-start | bytes 393220
  140.3 79.5 %copy-start.8 = (bf16[1,2048]{1,0:T(2,128)(2,1)S(1)}, bf16[1,2048]{1,0:T(2,128)(2,1)}, u32[]{:S(2)}) copy-start(bf16[1,2048]{1,0:T(2,128)(2,1)} %param.30) | copy-start | bytes 12292
  140.3 79.5 %copy-start.10 = (bf16[1,256]{1,0:T(2,128)(2,1)S(1)}, bf16[1,256]{1,0:T(2,128)(2,1)}, u32[]{:S(2)}) copy-start(bf16[1,256]{1,0:T(2,128)(2,1)} %param.31) | copy-start | bytes 1540
  213.5 60.6 %copy-start.3 = (bf16[64,1024]{1,0:T(8,128)(2,1)S(1)}, bf16[64,1024]{1,0:T(8,128)(2,1)}, u32[]{:S(2)}) copy-start(bf16[64,1024]{1,0:T(8,128)(2,1)} %param.37) | copy-start | bytes 393220
  216.2 12.0 %all-to-all-start = ((bf16[8,32,512]{2,1,0:T(8,128)(2,1)}), bf16[8,32,512]{2,1,0:T(8,128)(2,1)S(1)}, u32[]{:S(2)}, u32[]{:S(2)}) async-start(bf16[8,32,512]{2,1,0:T(8,128)(2,1)} %bitcast.24), calls=%async_computation | async-start | bytes 524288 | tf_op jit(solution)/shard_map/all_to_all | solution.py:181
  229.2 6.4 %collective-permute-start = (bf16[1,2048]{1,0:T(2,128)(2,1)S(1)}, bf16[1,2048]{1,0:T(2,128)(2,1)S(1)}, u32[]{:S(2)}, u32[]{:S(2)}) collective-permute-start(bf16[1,2048]{1,0:T(2,128)(2,1)S(1)} %convert_element_type.59), channel_id=1, source_target_pairs={{0,2},{2,4},{4,6},{6,8},{8,10},{10,12},{12,14},{14,0},{1,3},{3,5},... | collective-permute-start | bytes 12296 | tf_op jit(solution)/shard_map/ppermute | solution.py:201
  235.6 6.3 %collective-permute-start.1 = (bf16[1,2048]{1,0:T(2,128)(2,1)S(1)}, bf16[1,2048]{1,0:T(2,128)(2,1)S(1)}, u32[]{:S(2)}, u32[]{:S(2)}) collective-permute-start(bf16[1,2048]{1,0:T(2,128)(2,1)S(1)} %collective-permute-done), channel_id=1, source_target_pairs={{0,2},{2,4},{4,6},{6,8},{8,10},{10,12},{12,14},{14,0},{1,3},{3,5},... | collective-permute-start | bytes 12296 | tf_op jit(solution)/shard_map/ppermute | solution.py:201
  241.9 6.3 %collective-permute-start.2 = (bf16[1,2048]{1,0:T(2,128)(2,1)S(1)}, bf16[1,2048]{1,0:T(2,128)(2,1)S(1)}, u32[]{:S(2)}, u32[]{:S(2)}) collective-permute-start(bf16[1,2048]{1,0:T(2,128)(2,1)S(1)} %collective-permute-done.1), channel_id=1, source_target_pairs={{0,2},{2,4},{4,6},{6,8},{8,10},{10,12},{12,14},{14,0},{1,3},{3,5},... | collective-permute-start | bytes 12296 | tf_op jit(solution)/shard_map/ppermute | solution.py:201
  248.3 6.3 %collective-permute-start.3 = (bf16[1,2048]{1,0:T(2,128)(2,1)S(1)}, bf16[1,2048]{1,0:T(2,128)(2,1)S(1)}, u32[]{:S(2)}, u32[]{:S(2)}) collective-permute-start(bf16[1,2048]{1,0:T(2,128)(2,1)S(1)} %collective-permute-done.2), channel_id=1, source_target_pairs={{0,2},{2,4},{4,6},{6,8},{8,10},{10,12},{12,14},{14,0},{1,3},{3,5},... | collective-permute-start | bytes 12296 | tf_op jit(solution)/shard_map/ppermute | solution.py:201
  254.6 6.3 %collective-permute-start.4 = (bf16[1,2048]{1,0:T(2,128)(2,1)S(1)}, bf16[1,2048]{1,0:T(2,128)(2,1)S(1)}, u32[]{:S(2)}, u32[]{:S(2)}) collective-permute-start(bf16[1,2048]{1,0:T(2,128)(2,1)S(1)} %collective-permute-done.3), channel_id=1, source_target_pairs={{0,2},{2,4},{4,6},{6,8},{8,10},{10,12},{12,14},{14,0},{1,3},{3,5},... | collective-permute-start | bytes 12296 | tf_op jit(solution)/shard_map/ppermute | solution.py:201
  261.0 6.3 %collective-permute-start.5 = (bf16[1,2048]{1,0:T(2,128)(2,1)S(1)}, bf16[1,2048]{1,0:T(2,128)(2,1)S(1)}, u32[]{:S(2)}, u32[]{:S(2)}) collective-permute-start(bf16[1,2048]{1,0:T(2,128)(2,1)S(1)} %collective-permute-done.4), channel_id=1, source_target_pairs={{0,2},{2,4},{4,6},{6,8},{8,10},{10,12},{12,14},{14,0},{1,3},{3,5},... | collective-permute-start | bytes 12296 | tf_op jit(solution)/shard_map/ppermute | solution.py:201
  267.3 6.3 %collective-permute-start.6 = (bf16[1,2048]{1,0:T(2,128)(2,1)S(1)}, bf16[1,2048]{1,0:T(2,128)(2,1)S(1)}, u32[]{:S(2)}, u32[]{:S(2)}) collective-permute-start(bf16[1,2048]{1,0:T(2,128)(2,1)S(1)} %collective-permute-done.5), channel_id=1, source_target_pairs={{0,2},{2,4},{4,6},{6,8},{8,10},{10,12},{12,14},{14,0},{1,3},{3,5},... | collective-permute-start | bytes 12296 | tf_op jit(solution)/shard_map/ppermute | solution.py:201
Sparse Core Ops, SparseCore 0:
  9.5 51.7 all-gather.5
  63.4 71.3 all-gather.7
  136.9 71.3 all-gather.3
